TPU v7x, 1024 devices: a whole 8x8x8 slice. The times are simulated.
1024 devices in a mesh: lon: 64 (over y_lo, x, core), head: 16 (over y_hi, z).
Axes of the slice: x: 8, y: 8 (y_hi: 2, y_lo: 4; y = y_hi * 4 + y_lo), z: 8, core: 2. Of those that a mesh axis runs over, the one named last changes fastest.
Arguments:
- activations: bfloat16 [131072, 1024], P('lon')
- qkv_weight: bfloat16 [1024, 3072], P(None, 'head'), may hold values from -0.1875 to 0.1875
- attn_grad: bfloat16 [131072, 1024], P('lon', 'head'), may hold values from -6 to 6
- pos_bias: float32 [16, 128, 128], P('head'), may hold values from -4 to 4
- key_counts: int32 [1024], P('lon'), may hold values from 32 to 128, as said below
Outputs:
- input_grad: bfloat16 [131072, 1024], P(('lon', 'head'))
- weight_grad: float32 [1024, 3072], P(None, 'head')
Inputs may be any that keep to these rules, and one draw needn't show every extreme that they name: key_counts[g] is the number of valid keys of shifted window g; windows of window row 0 and of the last window row may hold fewer than 128, all others hold 128.
All inputs are finite; a program needn't handle non-finite values.
Results may differ from a plain program's by a relative error of at most 0.019.
The roundings to bfloat16 on the way count: a program that leaves them out, or rounds other values in their place, can miss the bound.
Values may be sent and summed in bfloat16 or wider, within the bound.
A program may use at most 64 MiB of HBM per device.

v0:
```python
import math

import jax
import jax.numpy as jnp
from jax import lax
from jax.sharding import PartitionSpec as P

HEAD_DIM = 64
WIN = 128
WIN_ROWS = 8
WIN_COLS = 2


def passed_along(shard, axis, by):
    size = lax.axis_size(axis)
    return lax.ppermute(shard, axis, [(i, (i + by) % size) for i in range(size)])


def assemble(block_grid, far_rows):
    first_part = block_grid[:, :, 1]
    second_part = jnp.concatenate([block_grid[:, 1:, 0], far_rows[:, None]], axis=1)
    return jnp.concatenate([first_part, second_part], axis=2)


def window_grads(proj_win, delta_win, pos_bias, valid_count):
    scale_factor = 1.0 / math.sqrt(proj_win.shape[-1])
    queries = proj_win[:, :, :, 0]
    keys_part = proj_win[:, :, :, 1]
    values_part = proj_win[:, :, :, 2]
    scores = (
        jnp.einsum("nqhe,nkhe->nhqk", queries, keys_part, preferred_element_type=jnp.float32)
        * scale_factor
        + pos_bias[None]
    )
    positions = jnp.arange(proj_win.shape[1], dtype=jnp.int32)
    valid_keys = positions[None, :] < valid_count[:, None]
    scores = jnp.where(valid_keys[:, None, None, :], scores, -jnp.inf)
    row_max = jnp.max(scores, axis=-1, keepdims=True)
    weights = jnp.exp(scores - row_max)
    probs = weights / jnp.sum(weights, axis=-1, keepdims=True)
    grad_probs = jnp.einsum(
        "nqhe,nkhe->nhqk", delta_win, values_part, preferred_element_type=jnp.float32
    )
    grad_scores = probs * (grad_probs - jnp.sum(probs * grad_probs, axis=-1, keepdims=True))
    probs_low = probs.astype(jnp.bfloat16)
    grads_low = grad_scores.astype(jnp.bfloat16)
    grad_values = jnp.einsum(
        "nhqk,nqhe->nkhe", probs_low, delta_win, preferred_element_type=jnp.float32
    )
    grad_queries = (
        jnp.einsum("nhqk,nkhe->nqhe", grads_low, keys_part, preferred_element_type=jnp.float32)
        * scale_factor
    )
    grad_keys = (
        jnp.einsum("nhqk,nqhe->nkhe", grads_low, queries, preferred_element_type=jnp.float32)
        * scale_factor
    )
    return jnp.stack([grad_queries, grad_keys, grad_values], axis=3).astype(jnp.bfloat16)


def shards(activations, qkv_weight, attn_grad, pos_bias, key_counts):
    heads_here = pos_bias.shape[0]
    width_all = qkv_weight.shape[1]
    delta_width = attn_grad.shape[1]
    half_len = WIN // 2
    projected = jnp.dot(activations, qkv_weight, preferred_element_type=jnp.float32).astype(
        jnp.bfloat16
    )
    proj_grid = projected.reshape(WIN_ROWS, WIN_COLS, 2, half_len, width_all)
    delta_grid = attn_grad.reshape(WIN_ROWS, WIN_COLS, 2, half_len, delta_width)
    outgoing = jnp.concatenate([proj_grid[:, 0, 0], delta_grid[:, 0, 0]], axis=2)
    incoming = passed_along(outgoing, "lon", -1)
    proj_win = assemble(proj_grid, incoming[:, :, :width_all])
    delta_win = assemble(delta_grid, incoming[:, :, width_all:])
    gradients = window_grads(
        proj_win.reshape(WIN_ROWS * WIN_COLS, WIN, heads_here, 3, HEAD_DIM),
        delta_win.reshape(WIN_ROWS * WIN_COLS, WIN, heads_here, HEAD_DIM),
        pos_bias,
        key_counts,
    ).reshape(WIN_ROWS, WIN_COLS, WIN, width_all)
    leading = gradients[:, :, :half_len]
    trailing = gradients[:, :, half_len:]
    returned = passed_along(trailing[:, WIN_COLS - 1], "lon", 1)
    first_halves = jnp.concatenate([returned[:, None], trailing[:, : WIN_COLS - 1]], axis=1)
    grad_proj = jnp.stack([first_halves, leading], axis=2).reshape(
        WIN_ROWS * WIN_COLS * WIN, width_all
    )
    local_grad = lax.dot_general(
        activations, grad_proj, (((0,), (0,)), ((), ())), preferred_element_type=jnp.float32
    )
    total_tokens = activations.shape[0] * lax.axis_size("lon")
    weight_grad = lax.psum(local_grad, "lon") / math.sqrt(total_tokens)
    partial_grad = lax.dot_general(
        grad_proj, qkv_weight, (((1,), (1,)), ((), ())), preferred_element_type=jnp.float32
    )
    partial_low = lax.optimization_barrier(partial_grad.astype(jnp.bfloat16)).astype(jnp.float32)
    input_grad = lax.psum_scatter(
        partial_low.astype(jnp.bfloat16), "head", scatter_dimension=0, tiled=True
    )
    return (input_grad, weight_grad)


def solution(mesh):
    placed = (P("lon", None), P(None, "head"), P("lon", "head"), P("head", None, None), P("lon"))
    return jax.shard_map(
        shards,
        mesh=mesh,
        in_specs=placed,
        out_specs=(P(("lon", "head"), None), P(None, "head")),
        check_vma=False,
    )
```

profile of v0, /device:TPU:1, one launch (start us, length us, event | category | flops | bytes accessed | tf_op | source)
XLA Modules:
  0.0 589.8 jit_solution(5463156811061741841)
XLA Ops:
  8.0 0.0 copy-start
  8.0 0.0 copy-start.1
  8.0 0.0 all-reduce.2.cloned.1.call-start
  8.1 0.9 copy-done
  9.0 3.7 convolution_convert_fusion.1
  12.7 0.5 copy.34
  13.2 0.0 copy-start.3
  13.3 0.0 copy-done.1
  13.3 0.5 reshape.131
  13.8 0.4 fusion.37
  14.2 0.2 copy.56
  14.4 0.8 pad_maximum_fusion.4
  15.2 16.1 %collective-permute-start = (bf16[8,64,256]{2,1,0:T(8,128)(2,1)}, bf16[8,64,256]{2,1,0:T(8,128)(2,1)S(1)}, u32[]{:S(2)}, u32[]{:S(2)}) collective-permute-start(bf16[8,64,256]{2,1,0:T(8,128)(2,1)} %pad_maximum_fusion.4), channel_id=1, source_target_pairs={{0,1008},{16,0},{32,16},{48,32},{64,48},{80,64},{96,80},{112,96},{... | collective-permute-start | bytes 786440 | tf_op jit(solution)/shard_map/ppermute | solution.py:16
  31.3 0.6 slice.68
  31.9 0.4 copy.35
  32.3 0.9 copy.40
  33.2 0.2 copy.59
  33.4 0.9 copy.41
  34.3 0.0 copy-done.3
  34.3 0.1 iota_compare_fusion
  34.4 0.0 collective-permute-done
  34.4 0.1 pad_maximum_fusion.2
  34.5 0.4 copy.37
  34.9 0.1 slice_bitcast_fusion.5
  35.0 0.1 pad_maximum_fusion.5
  35.1 0.2 copy.43
  35.2 0.9 fusion.38
  36.2 1.6 multiply_reduce_fusion
  37.8 0.0 copy-start.2
  37.8 0.2 multiply_convert_fusion
  38.0 0.3 fusion.9
  38.4 0.5 fusion.8
  38.9 0.0 copy-done.2
  38.9 0.5 fusion.7
  39.4 0.1 pad_maximum_fusion.1
  39.5 0.1 copy.49
  39.6 0.3 slice_bitcast_fusion.1
  39.9 1.9 collective-permute-start.1
  41.8 0.1 slice_bitcast_fusion
  41.9 4.6 collective-permute-done.1
  46.5 0.2 maximum_bitcast_fusion
  46.6 0.4 pad_maximum_fusion
  47.0 0.8 copy.51
  47.8 4.1 convolution_bitcast_fusion
  51.9 0.0 all-reduce.2.cloned.1.call-update
  51.9 0.0 reduce-scatter.2.cloned.1.call-start
  52.0 3.2 convolution_convert_fusion
  55.2 0.0 reduce-scatter.2.cloned.1.call-update
  55.2 525.0 %all-reduce.2.cloned.1.call-done = f32[1024,192]{0,1:T(8,128)} async-done(((f32[1024,192]{0,1:T(8,128)}), f32[1024,192]{0,1:T(8,128)}) %all-reduce.2.cloned.1.call-update) | async-done | bytes 786448 | tf_op jit(solution)/shard_map/psum | solution.py:92
  580.2 2.1 broadcast_multiply_fusion
  582.3 0.0 reduce-scatter.2.cloned.1.call-done
  (3 shorter events, 0.1 us)
Async XLA Ops:
  8.0 1.0 copy-start
  8.0 5.3 copy-start.1
  8.0 572.2 %all-reduce.2.cloned.1.call-start = ((), (), s32[]{:S(2)}) async-start(), calls=%async_computation.2 | async-start | bytes 1572864 | tf_op jit(solution)/shard_map/psum | solution.py:92
  13.2 21.1 %copy-start.3 = (s32[16]{0:T(128)S(1)}, s32[16]{0:T(128)}, u32[]{:S(2)}) copy-start(s32[16]{0:T(128)} %param.9) | copy-start | bytes 196
  15.2 19.2 %collective-permute-start = (bf16[8,64,256]{2,1,0:T(8,128)(2,1)}, bf16[8,64,256]{2,1,0:T(8,128)(2,1)S(1)}, u32[]{:S(2)}, u32[]{:S(2)}) collective-permute-start(bf16[8,64,256]{2,1,0:T(8,128)(2,1)} %pad_maximum_fusion.4), channel_id=1, source_target_pairs={{0,1008},{16,0},{32,16},{48,32},{64,48},{80,64},{96,80},{112,96},{... | collective-permute-start | bytes 786440 | tf_op jit(solution)/shard_map/ppermute | solution.py:16
  37.8 1.1 copy-start.2
  39.9 6.6 %collective-permute-start.1 = (bf16[8,64,192]{1,2,0:T(8,128)(2,1)S(1)}, bf16[8,64,192]{1,2,0:T(8,128)(2,1)S(1)}, u32[]{:S(2)}, u32[]{:S(2)}) collective-permute-start(bf16[8,64,192]{1,2,0:T(8,128)(2,1)S(1)} %get-tuple-element.4), channel_id=1, source_target_pairs={{0,16},{16,32},{32,48},{48,64},{64,80},{80,96},{96,112},{112,128},... | collective-permute-start | bytes 589832 | tf_op jit(solution)/shard_map/ppermute | solution.py:16
  51.9 530.4 %reduce-scatter.2.cloned.1.call-start = ((), (), s32[]{:S(2)}) async-start(), calls=%async_computation.1 | async-start | bytes 4456448 | tf_op jit(solution)/shard_map/reduce_scatter | solution.py:97
Sparse Core Ops, SparseCore 0:
  52.0 528.1 all-reduce.1
Sparse Core Ops, SparseCore 1:
  58.7 243.3 reduce-scatter.1
where the time goes:
time: 590 us
  waiting for transfers between devices  530 us (90%)
  starting transfers between devices  18.1 us (3%)
  between operations  15.7 us (3%)
  matrix products  14.9 us (3%)
  local copies, waits for them, and re-layouts  7.44 us (1%)
    psum x1, waiting for transfers between devices, shards(): weight_grad = lax.psum(local_grad, 'lon') / math.sqrt(total_tokens)  525 us
    ppermute x2, starting transfers between devices, passed_along(): lax.ppermute(shard, axis, [(i, (i + by) % size) for i in range(size)])  18 us
  transfers between devices with their start and end apart: 4, of which 2 were waited for; matrix products, arithmetic and copies ran while one was open for 1% of the time, Pallas kernels for 0%

commit v1 on v0

v1 whole, which is shorter than its diff:
```python
import math

import jax
import jax.numpy as jnp
from jax import lax
from jax.experimental import pallas as pl
from jax.experimental.pallas import tpu as pltpu
from jax.sharding import PartitionSpec as P

MESH = pl.DeviceIdType.MESH
F32 = jnp.float32
BF16 = jnp.bfloat16
D = 1024
HEAD_DIM = 64
WIN = 128
ROWS = 8
N_LON = 64
TOKENS = 131072
SCALE = 1.0 / math.sqrt(HEAD_DIM)
WG_SCALE = 1.0 / math.sqrt(TOKENS)
NT = (((1,), (1,)), ((), ()))
TN = (((0,), (0,)), ((), ()))
NN = (((1,), (0,)), ((), ()))


def dot(a, b, dims):
    return lax.dot_general(a, b, dims, preferred_element_type=F32)


def kernel(
    x_ref, wt_ref, a_ref, bias_ref, cnt_ref, out_ref, wg_ref,
    xs, ah, proj, biast, gpf, gps, gat, wgat, lhs, acc, ysend, yrecv,
    wacc, s_s, r_s, t_x, s_x, r_x, t_y, s_y, r_y, og,
    load_sem, own_sem, halo_s, halo_r, ahalo_s, ahalo_r, piece_s, piece_r,
    up_s, up_r, down_s, down_r, sib_s, sib_r, y_s, y_r,
    rss_s, rss_r, rsx_s, rsx_r, rsy_s, rsy_r, agy_s, agy_r, agx_s, agx_r, ags_s, ags_r,
):
    me_l = lax.axis_index("lon")
    me_h = lax.axis_index("head")
    yh, z = lax.div(me_h, 8), lax.rem(me_h, 8)
    core = lax.rem(me_l, 2)
    x = lax.rem(lax.div(me_l, 2), 8)
    yl = lax.div(me_l, 16)
    after = lax.rem(me_l + 1, N_LON)
    before = lax.rem(me_l + N_LON - 1, N_LON)
    sibling = me_l + 1 - 2 * core

    def remote(src, dst, send, recv, device):
        return pltpu.make_async_remote_copy(
            src_ref=src, dst_ref=dst, send_sem=send, recv_sem=recv, device_id=device, device_id_type=MESH
        )

    def z_peer(zz):
        return (me_l, yh * 8 + zz)

    def x_peer(i):
        return ((yl * 8 + lax.rem(x + i, 8)) * 2 + core, me_h)

    def y_peer(i):
        return ((lax.rem(yl + i, 4) * 8 + x) * 2 + core, me_h)

    partner = (me_l, (1 - yh) * 8 + z)

    load0 = pltpu.make_async_copy(x_ref.at[:, pl.ds(64, 128)], xs.at[:, pl.ds(0, 128)], load_sem.at[0])
    load1 = pltpu.make_async_copy(x_ref.at[:, pl.ds(192, 64)], xs.at[:, pl.ds(128, 64)], load_sem.at[1])
    load0.start()
    load1.start()
    own_w = pltpu.make_async_copy(wt_ref, wgat.at[z], own_sem)
    own_w.start()

    barrier = pltpu.get_barrier_semaphore()
    peers = [z_peer(lax.rem(z + i, 8)) for i in range(1, 8)]
    peers += [(near, yh * 8 + zz) for near in (after, before) for zz in range(8)]
    peers += [x_peer(i) for i in range(1, 8)] + [y_peer(i) for i in range(1, 4)] + [partner]
    for peer in peers:
        pl.semaphore_signal(barrier, inc=1, device_id=peer, device_id_type=MESH)
    pl.semaphore_wait(barrier, len(peers))

    def group(i):
        return 4 * lax.rem(1 - yh + i, 2)

    halo = [
        remote(
            x_ref.at[pl.ds(group(i), 4), pl.ds(0, 64)], xs.at[pl.ds(group(i), 4), pl.ds(192, 64)],
            halo_s.at[i], halo_r.at[i], (before, me_h),
        )
        for i in range(2)
    ]
    a_halo = remote(a_ref.at[:, pl.ds(0, 64)], ah, ahalo_s, ahalo_r, (before, me_h))
    a_halo.start()
    halo[0].start()
    halo[1].start()

    def up(k):
        slot = lax.rem(z + 8 - k, 8)
        src = wt_ref.at[core] if k == 0 else wgat.at[slot, core]
        return remote(src, wgat.at[slot, core], up_s.at[k], up_r.at[k], z_peer(lax.rem(z + 1, 8)))

    def down(k):
        slot = lax.rem(z + k, 8)
        src = wt_ref.at[core] if k == 0 else wgat.at[slot, core]
        return remote(src, wgat.at[slot, core], down_s.at[k], down_r.at[k], z_peer(lax.rem(z + 7, 8)))

    def to_sibling(n, slot):
        return remote(wgat.at[slot, core], wgat.at[slot, core], sib_s.at[n], sib_r.at[n], (sibling, me_h))

    up(0).start()
    down(0).start()

    def pump(k):
        up(k).wait_recv()
        if k < 3:
            up(k + 1).start()
        to_sibling(k, lax.rem(z + 7 - k, 8)).start()
        if k < 3:
            down(k).wait_recv()
            if k < 2:
                down(k + 1).start()
            to_sibling(4 + k, lax.rem(z + 1 + k, 8)).start()

    biast[...] = bias_ref[...].T

    def project(c, base):
        w = wt_ref[...].reshape(192, D)
        for j in range(0, 4, 2):
            rows = xs[pl.ds(base + j, 2), c * 128:(c + 1) * 128, :].reshape(256, D)
            proj[pl.ds(base + j, 2), c * 128:(c + 1) * 128, :] = (
                dot(rows, w, NT).astype(BF16).reshape(2, 128, 192)
            )

    def window(c, r):
        p = proj[r, c * 128:(c + 1) * 128, :]
        q, k, v = p[:, 0:64], p[:, 64:128], p[:, 128:192]
        if c == 0:
            a = a_ref[r, 64:192, :]
        else:
            a = jnp.concatenate([a_ref[r, 192:256, :], ah[r]], axis=0)
        scores = dot(k, q, NT) * SCALE + biast[...]
        position = lax.broadcasted_iota(jnp.int32, (WIN, WIN), 0)
        scores = jnp.where(position < cnt_ref[2 * r + c], scores, -jnp.inf)
        top = jnp.max(scores, axis=0, keepdims=True)
        weights = jnp.exp(scores - top)
        probs = weights / jnp.sum(weights, axis=0, keepdims=True)
        grad_probs = dot(v, a, NT)
        grads = probs * (grad_probs - jnp.sum(probs * grad_probs, axis=0, keepdims=True))
        probs_low = probs.astype(BF16)
        grads_low = grads.astype(BF16)
        dv = dot(probs_low, a, NN).astype(BF16)
        dk = dot(grads_low, q, NN) * SCALE
        dq = dot(grads_low, k, TN) * SCALE
        qk = jnp.concatenate([dq, dk], axis=1).astype(BF16)
        gpf[r, c * 128:(c + 1) * 128, 0:128] = qk
        gpf[r, c * 128:(c + 1) * 128, 128:192] = dv
        for half in range(2):
            lo = half * 64
            gps[r, 2 * c + half, 0:64, :] = qk[lo:lo + 64]
            gps[r, 2 * c + half, 64:96, :] = jnp.concatenate([dv[lo:lo + 32], dv[lo + 32:lo + 64]], axis=1)

    def piece(r, n):
        block = lax.rem(2 * r + (1 if n in (1, 2) else 0), 8)
        half = 1 if n in (0, 2) else 0
        src = gps.at[r, n]
        dst = gat.at[lax.div(r, 4), half, z]
        recv = piece_r.at[lax.div(r, 4), half, z]
        lon = after if n == 3 else me_l
        far = remote(src, dst, piece_s.at[r, n], recv, (lon, yh * 8 + block))
        near = None if n == 3 else pltpu.make_async_copy(src, dst, recv)
        return block, far, near

    def send_piece(r, n):
        block, far, near = piece(r, n)
        if near is None:
            far.start()
            return

        @pl.when(block == z)
        def _():
            near.start()

        @pl.when(block != z)
        def _():
            far.start()

    def attend(c, base):
        for j in range(4):
            window(c, base + j)
        for j in range(4):
            for half in range(2):
                send_piece(base + j, 2 * c + half)

    def weight_part(c):
        g = gpf[:, c * 128:(c + 1) * 128, :].reshape(1024, 192)
        for n in range(4):
            rows = xs[:, c * 128:(c + 1) * 128, n * 256:(n + 1) * 256].reshape(1024, 256)
            part = dot(g, rows, TN).reshape(2, 96, 256)
            if c == 0:
                wacc[:, :, n * 256:(n + 1) * 256] = part
            else:
                wacc[:, :, n * 256:(n + 1) * 256] += part

    load0.wait()
    for i in range(2):
        project(0, group(i))
        attend(0, group(i))
    weight_part(0)
    pump(0)
    load1.wait()
    a_halo.wait_recv()
    for i in range(2):
        halo[i].wait_recv()
        project(1, group(i))
        attend(1, group(i))
        if i == 0:
            pump(1)
    weight_part(1)

    s_s[...] = wacc[1 - core].astype(BF16)
    rss = remote(s_s, r_s, rss_s, rss_r, (sibling, me_h))
    rss.start()
    pump(2)
    rss.wait_recv()
    for i in range(8):
        cols = slice(i * 128, (i + 1) * 128)
        chunk = wacc[core, :, cols] + r_s[:, cols].astype(F32)
        t_x[i] = chunk
        s_x[i] = chunk.astype(BF16)
    rsx = [
        remote(s_x.at[lax.rem(x + i, 8)], r_x.at[i - 1], rsx_s.at[i - 1], rsx_r.at[i - 1], x_peer(i))
        for i in range(1, 8)
    ]
    for copy in rsx:
        copy.start()
    pump(3)
    for copy in rsx:
        copy.wait_recv()
    total = t_x[x]
    for i in range(7):
        total += r_x[i].astype(F32)
    for i in range(4):
        t_y[i] = total[i * 24:(i + 1) * 24]
        s_y[i] = total[i * 24:(i + 1) * 24].astype(BF16)
    rsy = [
        remote(s_y.at[lax.rem(yl + i, 4)], r_y.at[i - 1], rsy_s.at[i - 1], rsy_r.at[i - 1], y_peer(i))
        for i in range(1, 4)
    ]
    for copy in rsy:
        copy.start()

    own_w.wait()
    for n in range(7):
        to_sibling(n, 0).wait_recv()

    def gather(q):
        for half in range(2):
            for s in range(8):
                pltpu.make_async_copy(gps.at[0, 0], gat.at[q, half, s], piece_r.at[q, half, s]).wait()
        for s in range(8):
            for half in range(2):
                lo = half * 64
                lhs[s, lo:lo + 64, 0:128] = gat[q, half, s, 0:64, :]
                lhs[s, lo:lo + 32, 128:192] = gat[q, half, s, 64:96, 0:64]
                lhs[s, lo + 32:lo + 64, 128:192] = gat[q, half, s, 64:96, 64:128]

    def multiply(n):
        cols = slice(n * 256, (n + 1) * 256)
        total = None
        for s in range(8):
            part = dot(lhs[s], wgat[s, :, :, cols].reshape(192, 256), NN)
            total = part if total is None else total + part
        return total

    gather(1 - yh)
    for n in range(4):
        ysend[:, n * 256:(n + 1) * 256] = multiply(n).astype(BF16)
    exchange = remote(ysend, yrecv, y_s, y_r, partner)
    exchange.start()

    for copy in rsy:
        copy.wait_recv()
    total = t_y[yl]
    for i in range(3):
        total += r_y[i].astype(F32)
    og[core, x, yl] = (total * WG_SCALE).astype(BF16)
    mine = og.at[core, x, yl]
    agy = [remote(mine, mine, agy_s.at[i - 1], agy_r.at[i - 1], y_peer(i)) for i in range(1, 4)]
    for copy in agy:
        copy.start()

    gather(yh)
    for n in range(4):
        acc[:, n * 256:(n + 1) * 256] = multiply(n)

    for copy in agy:
        copy.wait_recv()
    mine_x = og.at[core, x]
    agx = [remote(mine_x, mine_x, agx_s.at[i - 1], agx_r.at[i - 1], x_peer(i)) for i in range(1, 8)]
    for copy in agx:
        copy.start()
    for copy in agx:
        copy.wait_recv()
    ags = remote(og.at[core], og.at[core], ags_s, ags_r, (sibling, me_h))
    ags.start()

    exchange.wait_recv()
    out_ref[...] = (acc[...] + yrecv[...].astype(F32)).astype(BF16)
    ags.wait_recv()
    for c in range(2):
        for i in range(8):
            for j in range(4):
                lo = c * 96 + j * 24
                wg_ref[lo:lo + 24, i * 128:(i + 1) * 128] = og[c, i, j].astype(F32)

    for k in range(4):
        up(k).wait_send()
    for k in range(3):
        down(k).wait_send()
    for n in range(7):
        to_sibling(n, 0).wait_send()
    a_halo.wait_send()
    for copy in halo:
        copy.wait_send()

    @pl.loop(0, ROWS)
    def _(r):
        for n in range(4):
            block, far, near = piece(r, n)
            if near is None:
                far.wait_send()
            else:

                @pl.when(block != z)
                def _():
                    far.wait_send()

    for copy in [rss, exchange, ags] + rsx + rsy + agy + agx:
        copy.wait_send()


def shards(activations, qkv_weight, attn_grad, pos_bias, key_counts):
    dma = pltpu.SemaphoreType.DMA
    vmem = pl.BlockSpec(memory_space=pltpu.VMEM)
    out, wg = pl.pallas_call(
        kernel,
        out_shape=(
            jax.ShapeDtypeStruct((128, D), BF16),
            jax.ShapeDtypeStruct((192, D), F32),
        ),
        in_specs=[
            pl.BlockSpec(memory_space=pl.ANY), vmem, vmem, vmem, pl.BlockSpec(memory_space=pltpu.SMEM),
        ],
        out_specs=(vmem, vmem),
        scratch_shapes=[
            pltpu.VMEM((8, 256, D), BF16),
            pltpu.VMEM((8, 64, 64), BF16),
            pltpu.VMEM((8, 256, 192), BF16),
            pltpu.VMEM((WIN, WIN), F32),
            pltpu.VMEM((8, 256, 192), BF16),
            pltpu.VMEM((8, 4, 96, 128), BF16),
            pltpu.VMEM((2, 2, 8, 96, 128), BF16),
            pltpu.VMEM((8, 2, 96, D), BF16),
            pltpu.VMEM((8, 128, 192), BF16),
            pltpu.VMEM((128, D), F32),
            pltpu.VMEM((128, D), BF16),
            pltpu.VMEM((128, D), BF16),
            pltpu.VMEM((2, 96, D), F32),
            pltpu.VMEM((96, D), BF16),
            pltpu.VMEM((96, D), BF16),
            pltpu.VMEM((8, 96, 128), F32),
            pltpu.VMEM((8, 96, 128), BF16),
            pltpu.VMEM((7, 96, 128), BF16),
            pltpu.VMEM((4, 24, 128), F32),
            pltpu.VMEM((4, 24, 128), BF16),
            pltpu.VMEM((3, 24, 128), BF16),
            pltpu.VMEM((2, 8, 4, 24, 128), BF16),
            dma((2,)), dma,
            dma((2,)), dma((2,)), dma, dma,
            dma((8, 4)), dma((2, 2, 8)),
            dma((4,)), dma((4,)), dma((3,)), dma((3,)),
            dma((7,)), dma((7,)), dma, dma,
            dma, dma, dma((7,)), dma((7,)), dma((3,)), dma((3,)),
            dma((3,)), dma((3,)), dma((7,)), dma((7,)), dma, dma,
        ],
        compiler_params=pltpu.CompilerParams(
            collective_id=0, has_side_effects=True, vmem_limit_bytes=48 * 1024 * 1024
        ),
    )(
        activations.reshape(ROWS, 256, D),
        qkv_weight.T.reshape(2, 96, D),
        attn_grad.reshape(ROWS, 256, HEAD_DIM),
        pos_bias[0],
        key_counts,
    )
    return out, wg.T


def solution(mesh):
    placed = (P("lon", None), P(None, "head"), P("lon", "head"), P("head", None, None), P("lon"))
    return jax.shard_map(
        shards,
        mesh=mesh,
        in_specs=placed,
        out_specs=(P(("lon", "head"), None), P(None, "head")),
        check_vma=False,
    )
```

time: 590 us -> 93.8 us (0.16)
  waiting for transfers between devices: 530 us -> 0 us
  Pallas kernels: 0 us -> 87.6 us
  starting transfers between devices: 18.1 us -> 0 us
  between operations: 15.7 us -> 0.66 us
  matrix products: 14.9 us -> 0 us
    psum x1 -> x0, waiting for transfers between devices: 525 us -> none  [shards(): weight_grad = lax.psum(local_grad, 'lon') / math.sqrt(total_tokens)]
    pallas_call x0 -> x1, Pallas kernels: none -> 87.6 us  [shards(): pl.pallas_call(kernel, out_shape=(jax.ShapeDtypeStruct((128, D), BF16), j...]
    ppermute x2 -> x0, starting transfers between devices: 18 us -> none  [passed_along(): lax.ppermute(shard, axis, [(i, (i + by) % size) for i in range(size)])]
    dot_general x7 -> x0, matrix products: 13.9 us -> none  [the longest x1 4.08 us: shards(): lax.dot_general(activations, grad_proj, (((0,), (0,)), ((), ())), preferr...]
  transfers between devices with their start and end apart: 4 -> 0, of which waited for: 2 -> 0; matrix products, arithmetic and copies ran while one was open for 1% -> 0% of each run, Pallas kernels for 0% -> 0%
where the time goes in v1:
time: 93.8 us; the launch traced here: 93.5 us
  Pallas kernels  87.6 us (93%)
  local copies, waits for them, and re-layouts  5.29 us (6%)
    pallas_call x1, Pallas kernels, shards(): pl.pallas_call(kernel, out_shape=(jax.ShapeDtypeStruct((128, D), BF16), j...  87.6 us
    unnamed x9, local copies, waits for them, and re-layouts  5.29 us

profile of v1, /device:TPU:1, one launch (start us, length us, event | category | flops | bytes accessed | tf_op | source)
XLA Modules:
  0.0 93.5 jit_solution(11503889466314995340)
XLA Ops:
  0.6 1.2 %copy.7 = bf16[2048,64]{1,0:T(8,128)(2,1)S(1)} copy(bf16[2048,64]{0,1:T(8,128)(2,1)} %param.7) | data formatting | bytes 524288 | tf_op args[2]
  1.9 0.0 copy-start
  1.9 1.0 %copy-done = bf16[1024,192]{0,1:T(8,128)(2,1)S(1)} copy-done((bf16[1024,192]{0,1:T(8,128)(2,1)S(1)}, bf16[1024,192]{0,1:T(8,128)(2,1)}, u32[]{:S(2)}) %copy-start) | copy-done | bytes 393240
  2.9 0.0 copy-start.1
  2.9 0.8 copy-done.1
  3.7 0.0 copy-start.2
  3.7 0.7 copy-done.2
  4.4 87.6 %shard_map.68 = (bf16[128,1024]{1,0:T(8,128)(2,1)S(1)}, f32[192,1024]{1,0:T(8,128)S(1)}) custom-call(bf16[8,256,1024]{2,1,0:T(8,128)(2,1)} %bitcast.11, bf16[2,96,1024]{2,1,0:T(8,128)(2,1)S(1)} %bitcast.9, bf16[8,256,64]{2,1,0:T(8,128)(2,1)S(1)} %bitcast.7, f32[128,128]{1,0:T(8,128)S(1)} %bitcast.10, s32[16]{0:T(128)S(1)} %copy-done.2), custom_call_target="tpu_custom_call" | custom-call | tf_op jit(solution)/shard_map/pallas_call | solution.py:342
  91.9 0.7 copy.10
  92.6 0.9 copy.11
Async XLA Ops:
  1.9 1.0 %copy-start = (bf16[1024,192]{0,1:T(8,128)(2,1)S(1)}, bf16[1024,192]{0,1:T(8,128)(2,1)}, u32[]{:S(2)}) copy-start(bf16[1024,192]{0,1:T(8,128)(2,1)} %param.6) | copy-start | bytes 1179652
  2.9 0.8 copy-start.1
  3.7 0.7 copy-start.2

commit v2 on v1

--- a/solution.py
+++ b/solution.py
@@ -28,12 +28,12 @@
 
 
 def kernel(
-    x_ref, wt_ref, a_ref, bias_ref, cnt_ref, out_ref, wg_ref,
-    xs, ah, proj, biast, gpf, gps, gat, wgat, lhs, acc, ysend, yrecv,
-    wacc, s_s, r_s, t_x, s_x, r_x, t_y, s_y, r_y, og,
+    x_ref, w_ref, at_ref, b_ref, c_ref, out_ref, wg_ref,
+    xs, wt_ref, at, a_ref, bias_ref, cnt_ref, ah, proj, biast, gpf, gps, gat, wgat, lhs, acc, ysend, yrecv,
+    wacc, s_s, r_s, t_x, s_x, r_x, r_y, og,
     load_sem, own_sem, halo_s, halo_r, ahalo_s, ahalo_r, piece_s, piece_r,
-    up_s, up_r, down_s, down_r, sib_s, sib_r, y_s, y_r,
-    rss_s, rss_r, rsx_s, rsx_r, rsy_s, rsy_r, agy_s, agy_r, agx_s, agx_r, ags_s, ags_r,
+    up_s, up_r, down_s, down_r, pair_s, pair_r, sib_s, sib_r, y_s, y_r,
+    rss_s, rss_r, rsx_s, rsx_r, rsy_s, rsy_r, agx_s, agx_r, ags_s, ags_r,
 ):
     me_l = lax.axis_index("lon")
     me_h = lax.axis_index("head")
@@ -44,6 +44,9 @@
     after = lax.rem(me_l + 1, N_LON)
     before = lax.rem(me_l + N_LON - 1, N_LON)
     sibling = me_l + 1 - 2 * core
+    odd = lax.rem(yl, 2)
+    mine, theirs = odd * 2 + core, (1 - odd) * 2 + core
+    pair = (me_l + 16 - 32 * odd, me_h)
 
     def remote(src, dst, send, recv, device):
         return pltpu.make_async_remote_copy(
@@ -63,10 +66,13 @@
 
     load0 = pltpu.make_async_copy(x_ref.at[:, pl.ds(64, 128)], xs.at[:, pl.ds(0, 128)], load_sem.at[0])
     load1 = pltpu.make_async_copy(x_ref.at[:, pl.ds(192, 64)], xs.at[:, pl.ds(128, 64)], load_sem.at[1])
-    load0.start()
-    load1.start()
-    own_w = pltpu.make_async_copy(wt_ref, wgat.at[z], own_sem)
-    own_w.start()
+    load_a = pltpu.make_async_copy(at_ref, at, load_sem.at[2])
+    load_w = pltpu.make_async_copy(w_ref, wt_ref, load_sem.at[3])
+    load_b = pltpu.make_async_copy(b_ref, bias_ref, load_sem.at[4])
+    load_c = pltpu.make_async_copy(c_ref, cnt_ref, load_sem.at[5])
+    own_w = pltpu.make_async_copy(w_ref, wgat.at[z], own_sem)
+    for copy in (load_a, load_w, load0, load_b, load_c, load1, own_w):
+        copy.start()
 
     barrier = pltpu.get_barrier_semaphore()
     peers = [z_peer(lax.rem(z + i, 8)) for i in range(1, 8)]
@@ -87,37 +93,57 @@
         for i in range(2)
     ]
     a_halo = remote(a_ref.at[:, pl.ds(0, 64)], ah, ahalo_s, ahalo_r, (before, me_h))
-    a_halo.start()
     halo[0].start()
     halo[1].start()
 
     def up(k):
         slot = lax.rem(z + 8 - k, 8)
-        src = wt_ref.at[core] if k == 0 else wgat.at[slot, core]
-        return remote(src, wgat.at[slot, core], up_s.at[k], up_r.at[k], z_peer(lax.rem(z + 1, 8)))
+        src = w_ref.at[mine] if k == 0 else wgat.at[slot, mine]
+        return remote(src, wgat.at[slot, mine], up_s.at[k], up_r.at[k], z_peer(lax.rem(z + 1, 8)))
 
     def down(k):
         slot = lax.rem(z + k, 8)
-        src = wt_ref.at[core] if k == 0 else wgat.at[slot, core]
-        return remote(src, wgat.at[slot, core], down_s.at[k], down_r.at[k], z_peer(lax.rem(z + 7, 8)))
-
-    def to_sibling(n, slot):
-        return remote(wgat.at[slot, core], wgat.at[slot, core], sib_s.at[n], sib_r.at[n], (sibling, me_h))
+        src = w_ref.at[mine] if k == 0 else wgat.at[slot, mine]
+        return remote(src, wgat.at[slot, mine], down_s.at[k], down_r.at[k], z_peer(lax.rem(z + 7, 8)))
+
+    def to_pair(n, slot):
+        return remote(wgat.at[slot, mine], wgat.at[slot, mine], pair_s.at[n], pair_r.at[n], pair)
+
+    def to_sibling(n, slot, part):
+        return remote(wgat.at[slot, part], wgat.at[slot, part], sib_s.at[n], sib_r.at[n], (sibling, me_h))
 
     up(0).start()
     down(0).start()
 
     def pump(k):
+        slot = lax.rem(z + 7 - k, 8)
         up(k).wait_recv()
         if k < 3:
             up(k + 1).start()
-        to_sibling(k, lax.rem(z + 7 - k, 8)).start()
+        to_pair(k, slot).start()
+        to_sibling(k, slot, mine).start()
         if k < 3:
+            slot = lax.rem(z + 1 + k, 8)
             down(k).wait_recv()
             if k < 2:
                 down(k + 1).start()
-            to_sibling(4 + k, lax.rem(z + 1 + k, 8)).start()
-
+            to_pair(4 + k, slot).start()
+            to_sibling(4 + k, slot, mine).start()
+
+    def pass_on(k):
+        slot = lax.rem(z + 7 - k, 8)
+        to_pair(k, slot).wait_recv()
+        to_sibling(7 + k, slot, theirs).start()
+        if k < 3:
+            slot = lax.rem(z + 1 + k, 8)
+            to_pair(4 + k, slot).wait_recv()
+            to_sibling(11 + k, slot, theirs).start()
+
+    load_a.wait()
+    for r in range(ROWS):
+        a_ref[r] = at[:, r * 256:(r + 1) * 256].T
+    a_halo.start()
+    load_b.wait()
     biast[...] = bias_ref[...].T
 
     def project(c, base):
@@ -184,9 +210,11 @@
     def attend(c, base):
         for j in range(4):
             window(c, base + j)
+
+    def send_group(base, pieces):
         for j in range(4):
-            for half in range(2):
-                send_piece(base + j, 2 * c + half)
+            for n in pieces:
+                send_piece(base + j, n)
 
     def weight_part(c):
         g = gpf[:, c * 128:(c + 1) * 128, :].reshape(1024, 192)
@@ -198,26 +226,36 @@
             else:
                 wacc[:, :, n * 256:(n + 1) * 256] += part
 
+    load_w.wait()
+    load_c.wait()
     load0.wait()
-    for i in range(2):
-        project(0, group(i))
-        attend(0, group(i))
+    project(0, group(0))
+    attend(0, group(0))
+    send_group(group(0), (0, 1))
+    pump(0)
+    project(0, group(1))
+    attend(0, group(1))
     weight_part(0)
-    pump(0)
     load1.wait()
     a_halo.wait_recv()
-    for i in range(2):
-        halo[i].wait_recv()
-        project(1, group(i))
-        attend(1, group(i))
-        if i == 0:
-            pump(1)
+    halo[0].wait_recv()
+    project(1, group(0))
+    pump(1)
+    attend(1, group(0))
+    send_group(group(0), (2, 3))
+    pass_on(0)
+    halo[1].wait_recv()
+    project(1, group(1))
+    pump(2)
+    attend(1, group(1))
     weight_part(1)
 
     s_s[...] = wacc[1 - core].astype(BF16)
     rss = remote(s_s, r_s, rss_s, rss_r, (sibling, me_h))
     rss.start()
-    pump(2)
+    pass_on(1)
+    pump(3)
+    send_group(group(1), range(4))
     rss.wait_recv()
     for i in range(8):
         cols = slice(i * 128, (i + 1) * 128)
@@ -230,25 +268,23 @@
     ]
     for copy in rsx:
         copy.start()
-    pump(3)
+    pass_on(2)
+    pass_on(3)
     for copy in rsx:
         copy.wait_recv()
     total = t_x[x]
     for i in range(7):
         total += r_x[i].astype(F32)
-    for i in range(4):
-        t_y[i] = total[i * 24:(i + 1) * 24]
-        s_y[i] = total[i * 24:(i + 1) * 24].astype(BF16)
+    r_y[yl] = total.astype(BF16)
     rsy = [
-        remote(s_y.at[lax.rem(yl + i, 4)], r_y.at[i - 1], rsy_s.at[i - 1], rsy_r.at[i - 1], y_peer(i))
-        for i in range(1, 4)
+        remote(r_y.at[yl], r_y.at[yl], rsy_s.at[i - 1], rsy_r.at[i - 1], y_peer(i)) for i in range(1, 4)
     ]
     for copy in rsy:
         copy.start()
 
     own_w.wait()
-    for n in range(7):
-        to_sibling(n, 0).wait_recv()
+    for n in range(14):
+        to_sibling(n, 0, 0).wait_recv()
 
     def gather(q):
         for half in range(2):
@@ -270,52 +306,55 @@
         return total
 
     gather(1 - yh)
+    exchange = [remote(ysend.at[n], yrecv.at[n], y_s.at[n], y_r.at[n], partner) for n in range(4)]
     for n in range(4):
-        ysend[:, n * 256:(n + 1) * 256] = multiply(n).astype(BF16)
-    exchange = remote(ysend, yrecv, y_s, y_r, partner)
-    exchange.start()
+        ysend[n] = multiply(n).astype(BF16)
+        exchange[n].start()
 
     for copy in rsy:
         copy.wait_recv()
-    total = t_y[yl]
-    for i in range(3):
+    total = r_y[0].astype(F32)
+    for i in range(1, 4):
         total += r_y[i].astype(F32)
-    og[core, x, yl] = (total * WG_SCALE).astype(BF16)
-    mine = og.at[core, x, yl]
-    agy = [remote(mine, mine, agy_s.at[i - 1], agy_r.at[i - 1], y_peer(i)) for i in range(1, 4)]
-    for copy in agy:
+    og[core, x] = (total * WG_SCALE).astype(BF16)
+    own = og.at[core, x]
+    agx = [remote(own, own, agx_s.at[i - 1], agx_r.at[i - 1], x_peer(i)) for i in range(1, 8)]
+    for copy in agx:
         copy.start()
+
+    def share(i):
+        part = og.at[core, lax.rem(x + 8 - i, 8)]
+        return remote(part, part, ags_s.at[i], ags_r.at[i], (sibling, me_h))
+
+    share(0).start()
 
     gather(yh)
     for n in range(4):
         acc[:, n * 256:(n + 1) * 256] = multiply(n)
 
-    for copy in agy:
-        copy.wait_recv()
-    mine_x = og.at[core, x]
-    agx = [remote(mine_x, mine_x, agx_s.at[i - 1], agx_r.at[i - 1], x_peer(i)) for i in range(1, 8)]
-    for copy in agx:
-        copy.start()
-    for copy in agx:
-        copy.wait_recv()
-    ags = remote(og.at[core], og.at[core], ags_s, ags_r, (sibling, me_h))
-    ags.start()
-
-    exchange.wait_recv()
-    out_ref[...] = (acc[...] + yrecv[...].astype(F32)).astype(BF16)
-    ags.wait_recv()
+    for i in range(1, 8):
+        agx[i - 1].wait_recv()
+        share(i).start()
+    for n in range(4):
+        cols = slice(n * 256, (n + 1) * 256)
+        exchange[n].wait_recv()
+        out_ref[:, cols] = (acc[:, cols] + yrecv[n].astype(F32)).astype(BF16)
+    for i in range(8):
+        share(i).wait_recv()
     for c in range(2):
         for i in range(8):
-            for j in range(4):
-                lo = c * 96 + j * 24
-                wg_ref[lo:lo + 24, i * 128:(i + 1) * 128] = og[c, i, j].astype(F32)
+            wg_ref[c * 96:(c + 1) * 96, i * 128:(i + 1) * 128] = og[c, i].astype(F32)
 
     for k in range(4):
         up(k).wait_send()
     for k in range(3):
         down(k).wait_send()
     for n in range(7):
-        to_sibling(n, 0).wait_send()
+        to_pair(n, 0).wait_send()
+    for n in range(14):
+        to_sibling(n, 0, 0).wait_send()
+    for i in range(8):
+        share(i).wait_send()
     a_halo.wait_send()
     for copy in halo:
         copy.wait_send()
@@ -332,13 +371,14 @@
                 def _():
                     far.wait_send()
 
-    for copy in [rss, exchange, ags] + rsx + rsy + agy + agx:
+    for copy in [rss] + exchange + rsx + rsy + agx:
         copy.wait_send()
 
 
 def shards(activations, qkv_weight, attn_grad, pos_bias, key_counts):
     dma = pltpu.SemaphoreType.DMA
     vmem = pl.BlockSpec(memory_space=pltpu.VMEM)
+    hbm = pl.BlockSpec(memory_space=pltpu.MemorySpace.HBM)
     out, wg = pl.pallas_call(
         kernel,
         out_shape=(
@@ -346,47 +386,51 @@
             jax.ShapeDtypeStruct((192, D), F32),
         ),
         in_specs=[
-            pl.BlockSpec(memory_space=pl.ANY), vmem, vmem, vmem, pl.BlockSpec(memory_space=pltpu.SMEM),
+            hbm, hbm, hbm,
+            hbm, hbm,
         ],
         out_specs=(vmem, vmem),
         scratch_shapes=[
             pltpu.VMEM((8, 256, D), BF16),
+            pltpu.VMEM((4, 48, D), BF16),
+            pltpu.VMEM((64, 2048), BF16),
+            pltpu.VMEM((8, 256, 64), BF16),
+            pltpu.VMEM((WIN, WIN), F32),
+            pltpu.SMEM((16,), jnp.int32),
             pltpu.VMEM((8, 64, 64), BF16),
             pltpu.VMEM((8, 256, 192), BF16),
             pltpu.VMEM((WIN, WIN), F32),
             pltpu.VMEM((8, 256, 192), BF16),
             pltpu.VMEM((8, 4, 96, 128), BF16),
             pltpu.VMEM((2, 2, 8, 96, 128), BF16),
-            pltpu.VMEM((8, 2, 96, D), BF16),
+            pltpu.VMEM((8, 4, 48, D), BF16),
             pltpu.VMEM((8, 128, 192), BF16),
             pltpu.VMEM((128, D), F32),
-            pltpu.VMEM((128, D), BF16),
-            pltpu.VMEM((128, D), BF16),
+            pltpu.VMEM((4, 128, 256), BF16),
+            pltpu.VMEM((4, 128, 256), BF16),
             pltpu.VMEM((2, 96, D), F32),
             pltpu.VMEM((96, D), BF16),
             pltpu.VMEM((96, D), BF16),
             pltpu.VMEM((8, 96, 128), F32),
             pltpu.VMEM((8, 96, 128), BF16),
             pltpu.VMEM((7, 96, 128), BF16),
-            pltpu.VMEM((4, 24, 128), F32),
-            pltpu.VMEM((4, 24, 128), BF16),
-            pltpu.VMEM((3, 24, 128), BF16),
-            pltpu.VMEM((2, 8, 4, 24, 128), BF16),
-            dma((2,)), dma,
+            pltpu.VMEM((4, 96, 128), BF16),
+            pltpu.VMEM((2, 8, 96, 128), BF16),
+            dma((6,)), dma,
             dma((2,)), dma((2,)), dma, dma,
             dma((8, 4)), dma((2, 2, 8)),
-            dma((4,)), dma((4,)), dma((3,)), dma((3,)),
-            dma((7,)), dma((7,)), dma, dma,
+            dma((4,)), dma((4,)), dma((3,)), dma((3,)), dma((7,)), dma((7,)),
+            dma((14,)), dma((14,)), dma((4,)), dma((4,)),
             dma, dma, dma((7,)), dma((7,)), dma((3,)), dma((3,)),
-            dma((3,)), dma((3,)), dma((7,)), dma((7,)), dma, dma,
+            dma((7,)), dma((7,)), dma((8,)), dma((8,)),
         ],
         compiler_params=pltpu.CompilerParams(
-            collective_id=0, has_side_effects=True, vmem_limit_bytes=48 * 1024 * 1024
+            collective_id=0, has_side_effects=True, vmem_limit_bytes=60 * 1024 * 1024
         ),
     )(
         activations.reshape(ROWS, 256, D),
-        qkv_weight.T.reshape(2, 96, D),
-        attn_grad.reshape(ROWS, 256, HEAD_DIM),
+        qkv_weight.T.reshape(4, 48, D),
+        attn_grad.T,
         pos_bias[0],
         key_counts,
     )

time: 93.8 us -> 84.7 us (0.903)
  Pallas kernels: 87.6 us -> 80.1 us
  local copies, waits for them, and re-layouts: 5.29 us -> 3.76 us
    pallas_call x1, Pallas kernels: 87.6 us -> 80.1 us  [shards(): pl.pallas_call(kernel, out_shape=(jax.ShapeDtypeStruct((128, D), BF16), j...]
    unnamed x9 -> x2, local copies, waits for them, and re-layouts: 5.29 us -> 3.76 us
where the time goes in v2:
time: 84.7 us; the launch traced here: 84.5 us
  Pallas kernels  80.1 us (95%)
  local copies, waits for them, and re-layouts  3.76 us (4%)
    pallas_call x1, Pallas kernels, shards(): pl.pallas_call(kernel, out_shape=(jax.ShapeDtypeStruct((128, D), BF16), j...  80.1 us
    unnamed x2, local copies, waits for them, and re-layouts  3.76 us

profile of v2, /device:TPU:1, one launch (start us, length us, event | category | flops | bytes accessed | tf_op | source)
XLA Modules:
  0.0 84.5 jit_solution(7106395580726204655)
XLA Ops:
  0.6 80.1 %shard_map.68 = (bf16[128,1024]{1,0:T(8,128)(2,1)}, f32[192,1024]{1,0:T(8,128)}) custom-call(bf16[8,256,1024]{2,1,0:T(8,128)(2,1)} %bitcast.7, bf16[4,48,1024]{2,1,0:T(8,128)(2,1)} %bitcast.9, bf16[64,2048]{1,0:T(8,128)(2,1)} %bitcast.10, f32[128,128]{1,0:T(8,128)} %bitcast.11, s32[16]{0:T(128)} %c_ref.1), custom_call_target="tpu_custom_call" | custom-call | tf_op jit(solution)/shard_map/pallas_call | solution.py:382
  80.7 1.7 %copy.9 = bf16[128,1024]{1,0:T(8,128)(2,1)} copy(bf16[128,1024]{1,0:T(8,128)(2,1)} %get-tuple-element.8) | data formatting | bytes 524288
  82.4 2.1 %copy.10 = f32[1024,192]{0,1:T(8,128)} copy(f32[1024,192]{0,1:T(8,128)} %bitcast.8) | data formatting | bytes 1572864

commit v3 on v2

--- a/solution.py
+++ b/solution.py
@@ -97,14 +97,14 @@
     halo[1].start()
 
     def up(k):
-        slot = lax.rem(z + 8 - k, 8)
-        src = w_ref.at[mine] if k == 0 else wgat.at[slot, mine]
-        return remote(src, wgat.at[slot, mine], up_s.at[k], up_r.at[k], z_peer(lax.rem(z + 1, 8)))
+        slot = z if k < 2 else lax.rem(z + 6, 8)
+        src = w_ref.at[mine] if k < 2 else wgat.at[slot, mine]
+        return remote(src, wgat.at[slot, mine], up_s.at[k], up_r.at[k], z_peer(lax.rem(z + 1 + k % 2, 8)))
 
     def down(k):
-        slot = lax.rem(z + k, 8)
-        src = w_ref.at[mine] if k == 0 else wgat.at[slot, mine]
-        return remote(src, wgat.at[slot, mine], down_s.at[k], down_r.at[k], z_peer(lax.rem(z + 7, 8)))
+        slot = z if k < 2 else lax.rem(z + 2, 8)
+        src = w_ref.at[mine] if k < 2 else wgat.at[slot, mine]
+        return remote(src, wgat.at[slot, mine], down_s.at[k], down_r.at[k], z_peer(lax.rem(z + 7 - k % 2, 8)))
 
     def to_pair(n, slot):
         return remote(wgat.at[slot, mine], wgat.at[slot, mine], pair_s.at[n], pair_r.at[n], pair)
@@ -112,21 +112,23 @@
     def to_sibling(n, slot, part):
         return remote(wgat.at[slot, part], wgat.at[slot, part], sib_s.at[n], sib_r.at[n], (sibling, me_h))
 
-    up(0).start()
-    down(0).start()
+    for k in (1, 0):
+        up(k).start()
+        down(k).start()
 
     def pump(k):
         slot = lax.rem(z + 7 - k, 8)
         up(k).wait_recv()
-        if k < 3:
-            up(k + 1).start()
+        if k == 1:
+            up(3).start()
+            up(2).start()
         to_pair(k, slot).start()
         to_sibling(k, slot, mine).start()
         if k < 3:
             slot = lax.rem(z + 1 + k, 8)
             down(k).wait_recv()
-            if k < 2:
-                down(k + 1).start()
+            if k == 1:
+                down(2).start()
             to_pair(4 + k, slot).start()
             to_sibling(4 + k, slot, mine).start()
 
@@ -232,10 +234,10 @@
     project(0, group(0))
     attend(0, group(0))
     send_group(group(0), (0, 1))
-    pump(0)
     project(0, group(1))
     attend(0, group(1))
     weight_part(0)
+    pump(0)
     load1.wait()
     a_halo.wait_recv()
     halo[0].wait_recv()
@@ -246,7 +248,6 @@
     pass_on(0)
     halo[1].wait_recv()
     project(1, group(1))
-    pump(2)
     attend(1, group(1))
     weight_part(1)
 
@@ -254,6 +255,7 @@
     rss = remote(s_s, r_s, rss_s, rss_r, (sibling, me_h))
     rss.start()
     pass_on(1)
+    pump(2)
     pump(3)
     send_group(group(1), range(4))
     rss.wait_recv()
@@ -341,9 +343,7 @@
         out_ref[:, cols] = (acc[:, cols] + yrecv[n].astype(F32)).astype(BF16)
     for i in range(8):
         share(i).wait_recv()
-    for c in range(2):
-        for i in range(8):
-            wg_ref[c * 96:(c + 1) * 96, i * 128:(i + 1) * 128] = og[c, i].astype(F32)
+    wg_ref[...] = og[...]
 
     for k in range(4):
         up(k).wait_send()
@@ -375,6 +375,13 @@
         copy.wait_send()
 
 
+def finish(part_ref, og_ref, out_ref, wg_ref):
+    out_ref[...] = part_ref[...]
+    for c in range(2):
+        for i in range(8):
+            wg_ref[c * 96:(c + 1) * 96, i * 128:(i + 1) * 128] = og_ref[c, i].astype(F32)
+
+
 def shards(activations, qkv_weight, attn_grad, pos_bias, key_counts):
     dma = pltpu.SemaphoreType.DMA
     vmem = pl.BlockSpec(memory_space=pltpu.VMEM)
@@ -383,7 +390,7 @@
         kernel,
         out_shape=(
             jax.ShapeDtypeStruct((128, D), BF16),
-            jax.ShapeDtypeStruct((192, D), F32),
+            jax.ShapeDtypeStruct((2, 8, 96, 128), BF16),
         ),
         in_specs=[
             hbm, hbm, hbm,
@@ -434,6 +441,13 @@
         pos_bias[0],
         key_counts,
     )
+    out, wg = pl.pallas_call(
+        finish,
+        out_shape=(jax.ShapeDtypeStruct((128, D), BF16), jax.ShapeDtypeStruct((192, D), F32)),
+        in_specs=[vmem, vmem],
+        out_specs=(vmem, vmem),
+        compiler_params=pltpu.CompilerParams(vmem_limit_bytes=60 * 1024 * 1024),
+    )(out, wg)
     return out, wg.T
 
 

time: 84.7 us -> 81.7 us (0.965)
  local copies, waits for them, and re-layouts: 3.76 us -> 0 us
    unnamed x2 -> x0, local copies, waits for them, and re-layouts: 3.76 us -> none
    pallas_call x0 -> x1, Pallas kernels: none -> 2.06 us  [shards(): pl.pallas_call(finish, out_shape=(jax.ShapeDtypeStruct((128, D), BF16), j...]
    pallas_call x1, Pallas kernels: 80.1 us -> 78.3 us  [shards(): pl.pallas_call(kernel, out_shape=(jax.ShapeDtypeStruct((128, D), BF16), j...]
where the time goes in v3:
time: 81.7 us; the launch traced here: 81 us
  Pallas kernels  80.3 us (98%)
    pallas_call x1, Pallas kernels, shards(): pl.pallas_call(kernel, out_shape=(jax.ShapeDtypeStruct((128, D), BF16), j...  78.3 us
    pallas_call x1, Pallas kernels, shards(): pl.pallas_call(finish, out_shape=(jax.ShapeDtypeStruct((128, D), BF16), j...  2.06 us

profile of v3, /device:TPU:1, one launch (start us, length us, event | category | flops | bytes accessed | tf_op | source)
XLA Modules:
  0.0 81.0 jit_solution(10916159361335936966)
XLA Ops:
  0.6 78.3 %shard_map.68 = (bf16[128,1024]{1,0:T(8,128)(2,1)}, bf16[2,8,96,128]{3,2,1,0:T(8,128)(2,1)}) custom-call(bf16[8,256,1024]{2,1,0:T(8,128)(2,1)} %bitcast.7, bf16[4,48,1024]{2,1,0:T(8,128)(2,1)} %bitcast.8, bf16[64,2048]{1,0:T(8,128)(2,1)} %bitcast.9, f32[128,128]{1,0:T(8,128)} %bitcast.10, s32[16]{0:T(128)} %c_ref.1), custom_call_target="tpu_custom_call" | custom-call | tf_op jit(solution)/shard_map/pallas_call | solution.py:389
  78.9 2.1 %shard_map.69 = (bf16[128,1024]{1,0:T(8,128)(2,1)}, f32[192,1024]{1,0:T(8,128)}) custom-call(bf16[128,1024]{1,0:T(8,128)(2,1)} %get-tuple-element.6.part_ref, bf16[2,8,96,128]{3,2,1,0:T(8,128)(2,1)} %get-tuple-element.7.og_ref), custom_call_target="tpu_custom_call" | custom-call | tf_op jit(solution)/shard_map/pallas_call | solution.py:444
